TPU v7x, 256 devices: a whole 4x4x8 slice. The times are simulated.
256 devices in a mesh: seq: 32 (over z, y), head: 2 (over core), dp: 4 (over x).
Axes of the slice: x: 4, y: 4, z: 8, core: 2. Of those that a mesh axis runs over, the one named last changes fastest.
Arguments:
- series: bfloat16 [4, 16384, 768], P('dp', 'seq'), may hold values from -6 to 6
- norm_attn: float32 [768], replicated, may hold values from 0.1 to 1.9
- qkv_weight: bfloat16 [768, 3, 768], P(None, None, 'head'), may hold values from -0.21875 to 0.21875
- out_weight: bfloat16 [768, 768], P('head'), may hold values from -0.21875 to 0.21875
- norm_moe: float32 [768], replicated, may hold values from 0.1 to 1.9
- router_weight: bfloat16 [768, 128], replicated, may hold values from -0.21875 to 0.21875
- expert_ids: int32 [4, 16384, 1], P('dp', ('seq', 'head')), may hold values from 0 to 127; in each aligned block of 256 rows (0 to 255, 256 to 511, ..., all dimensions but the last counted through in order) at most 4 rows name the same one
- gate_weight: bfloat16 [128, 768, 3072], P(('seq', 'dp'), None, 'head'), may hold values from -0.21875 to 0.21875
- up_weight: bfloat16 [128, 768, 3072], P(('seq', 'dp'), None, 'head'), may hold values from -0.21875 to 0.21875
- down_weight: bfloat16 [128, 3072, 768], P(('seq', 'dp'), 'head'), may hold values from -0.109375 to 0.109375
Outputs:
- layer_out: bfloat16 [4, 16384, 768], P('dp', ('seq', 'head'))
Inputs may be any that keep to these rules, and one draw needn't show every extreme that they name: `expert_ids`: among the rows of one device (aligned blocks of 256 positions, counted over series and positions in order) at most 4 name the same expert, and in every draw some expert is named by exactly 4 rows of some device.
All inputs are finite; a program needn't handle non-finite values.
Results may differ from a plain program's by a relative error of at most 0.0041.
Values may be sent and summed in bfloat16 or wider, within the bound.
No kernel may reach another device: no remote copies, remote signals or barrier semaphores. Data moves between devices by JAX's collectives and lax.ppermute only.
A program may use at most 128 MiB of HBM per device.

v0:
```python
import math

import jax
import jax.numpy as jnp
from jax import lax
from jax.experimental import pallas as pl
from jax.experimental.pallas import tpu as pltpu
from jax.sharding import Mesh
from jax.sharding import PartitionSpec as P


HD = 128
SEQ = ("seq_0", "seq_1")
SEQ_DP = ("seq_0", "seq_1", "dp")
SEQ_HEAD = ("seq_0", "seq_1", "head")
NORM_EPS = 1e-06
FF_BLOCK = 512
MIB = 1024 * 1024


def from_partner(shard):
    return lax.ppermute(shard, "head", [(0, 1), (1, 0)])


def exchange(pieces, axes):
    return lax.all_to_all(pieces, axes, split_axis=0, concat_axis=0, tiled=True)


def expert_kernel(rows, gate_a, up_a, down_a, gate_b, up_b, down_b, out, gate, up, down, total, sems):
    blocks = gate.shape[0]
    own_blocks = blocks // 2
    first = FF_BLOCK // 2

    def copies(k):
        gates, ups, downs = (gate_a, up_a, down_a) if k < own_blocks else (gate_b, up_b, down_b)
        base = (k % own_blocks) * FF_BLOCK
        spans = ((0, first), (first, first)) if k == 0 else ((0, FF_BLOCK),)
        for n, (at, size) in enumerate(spans):
            row = 0 if k == 0 and n == 0 else k + 1
            to, source = pl.ds(at, size), pl.ds(base + at, size)
            yield pltpu.make_async_copy(gates.at[:, source], gate.at[k, :, to], sems.at[row, 0])
            yield pltpu.make_async_copy(ups.at[:, source], up.at[k, :, to], sems.at[row, 1])
            yield pltpu.make_async_copy(downs.at[source, :], down.at[k, to, :], sems.at[row, 2])

    started = [list(copies(k)) for k in range(blocks)]
    for some in started:
        for copy in some:
            copy.start()

    def part(gates, ups, downs):
        x = rows[...]
        g = jnp.dot(x, gates, preferred_element_type=jnp.float32)
        u = jnp.dot(x, ups, preferred_element_type=jnp.float32)
        hidden = (g * (0.5 + 0.5 * jnp.tanh(0.5 * g)) * u).astype(jnp.bfloat16)
        return jnp.dot(hidden, downs, preferred_element_type=jnp.float32)

    for copy in started[0][:3]:
        copy.wait()
    total[...] = part(gate[0, :, :first], up[0, :, :first], down[0, :first, :])
    for copy in started[0][3:]:
        copy.wait()
    total[...] += part(gate[0, :, first:], up[0, :, first:], down[0, first:, :])

    def step(k, carry):
        whole = pl.ds(0, FF_BLOCK)
        pltpu.make_async_copy(gate_a.at[:, whole], gate.at[k], sems.at[k + 1, 0]).wait()
        pltpu.make_async_copy(up_a.at[:, whole], up.at[k], sems.at[k + 1, 1]).wait()
        pltpu.make_async_copy(down_a.at[whole, :], down.at[k], sems.at[k + 1, 2]).wait()
        total[...] += part(gate[k], up[k], down[k])
        return carry

    lax.fori_loop(1, blocks, step, 0)
    out[...] = total[...].astype(out.dtype)


def expert_of(rows, own, partner):
    count, width = rows.shape
    units = own[0].shape[1]
    blocks = 2 * units // FF_BLOCK
    local = pl.BlockSpec(memory_space=pltpu.VMEM)
    return pl.pallas_call(
        expert_kernel,
        in_specs=[local] + [pl.BlockSpec(memory_space=pl.ANY)] * 6,
        out_specs=local,
        out_shape=jax.ShapeDtypeStruct((count, width), jnp.bfloat16),
        scratch_shapes=[
            pltpu.VMEM((blocks, width, FF_BLOCK), jnp.bfloat16),
            pltpu.VMEM((blocks, width, FF_BLOCK), jnp.bfloat16),
            pltpu.VMEM((blocks, FF_BLOCK, width), jnp.bfloat16),
            pltpu.VMEM((count, width), jnp.float32),
            pltpu.SemaphoreType.DMA((blocks + 1, 3)),
        ],
        compiler_params=pltpu.CompilerParams(vmem_limit_bytes=36 * MIB),
        cost_estimate=pl.CostEstimate(
            flops=2 * count * width * units * 6,
            bytes_accessed=12 * width * units,
            transcendentals=2 * count * units,
        ),
        name="expert_mlp",
    )(rows, *(in_hbm(w) for w in own), *(in_hbm(w) for w in partner))


def in_parts(source, target, sems, parts):
    size = source.shape[0] // parts
    return [
        pltpu.make_async_copy(
            source.at[pl.ds(k * size, size)], target.at[pl.ds(k * size, size)], sems.at[k]
        )
        for k in range(parts)
    ]


def in_hbm(array):
    return pltpu.with_memory_space_constraint(array, pltpu.HBM)


def in_vmem(array):
    return pltpu.with_memory_space_constraint(array, pltpu.VMEM)


def normed_rows(rows, gain):
    x = rows.astype(jnp.float32)
    mean = jnp.sum(x * x, axis=-1, keepdims=True) * (1.0 / x.shape[1])
    return x * lax.rsqrt(mean + NORM_EPS) * gain.reshape(1, -1)


def state_kernel(series, weight, gain, state_out, normed_out, rows, table, gain_in, sems):
    half = weight.shape[2]
    fetches = [in_parts(series, rows, sems.at[0], 4)] + [
        in_parts(weight.at[k], table.at[:, pl.ds((k - 1) * half, half)], sems.at[k], 4)
        for k in (1, 2)
    ]
    fetch_gain = pltpu.make_async_copy(gain, gain_in, sems.at[3, 0])
    for fetch in fetches[0]:
        fetch.start()
    fetch_gain.start()
    for some in fetches[1:]:
        for fetch in some:
            fetch.start()
    fetch_gain.wait()
    size = rows.shape[0] // len(fetches[0])
    for k, fetch in enumerate(fetches[0]):
        at = slice(k * size, (k + 1) * size)
        fetch.wait()
        normed_out[at, :] = normed_rows(rows[at, :], gain_in[...]).astype(jnp.bfloat16)
    for some in fetches[1:]:
        for fetch in some:
            fetch.wait()
    both = jnp.dot(normed_out[...], table[...], preferred_element_type=jnp.float32)
    both = both.astype(jnp.bfloat16)
    heads = half // HD
    for n in range(heads):
        at = slice(n * HD, (n + 1) * HD)
        state_out[at, :] = lax.dot_general(
            both[:, n * HD : (n + 1) * HD],
            both[:, half + n * HD : half + (n + 1) * HD],
            (((0,), (0,)), ((), ())),
            preferred_element_type=jnp.float32,
        ).astype(jnp.bfloat16)
    state_out[heads * HD :, :] = jnp.zeros((HD, HD), jnp.bfloat16)


def block_state(series, weight, gain):
    count, width = series.shape
    half = weight.shape[2]
    return pl.pallas_call(
        state_kernel,
        in_specs=[
            pl.BlockSpec(memory_space=pl.ANY),
            pl.BlockSpec(memory_space=pl.ANY),
            pl.BlockSpec(memory_space=pl.ANY),
        ],
        out_specs=[pl.BlockSpec(memory_space=pltpu.VMEM)] * 2,
        out_shape=[
            jax.ShapeDtypeStruct((half + HD, HD), jnp.bfloat16),
            pltpu.VMEM((count, width), jnp.bfloat16),
        ],
        scratch_shapes=[
            pltpu.VMEM((count, width), jnp.bfloat16),
            pltpu.VMEM((width, 2 * half), jnp.bfloat16),
            pltpu.VMEM((width,), jnp.float32),
            pltpu.SemaphoreType.DMA((4, 4)),
        ],
        compiler_params=pltpu.CompilerParams(vmem_limit_bytes=24 * MIB),
        cost_estimate=pl.CostEstimate(
            flops=4 * count * width * half, bytes_accessed=4 * count * width, transcendentals=count
        ),
        name="block_state",
    )(in_hbm(series), in_hbm(weight), in_hbm(gain))


def prefix_kernel(pieces, out):
    total = jnp.zeros(pieces.shape[1:], jnp.float32)
    for k in range(pieces.shape[0]):
        rounded = total.astype(jnp.bfloat16)
        out[k] = rounded
        total = total + pieces[k].astype(jnp.float32)


def prefix(pieces):
    count, lines, lanes = pieces.shape
    return pl.pallas_call(
        prefix_kernel,
        in_specs=[pl.BlockSpec(memory_space=pltpu.VMEM)],
        out_specs=pl.BlockSpec(memory_space=pltpu.VMEM),
        out_shape=jax.ShapeDtypeStruct((count, lines, lanes), jnp.bfloat16),
        compiler_params=pltpu.CompilerParams(vmem_limit_bytes=4 * MIB),
        cost_estimate=pl.CostEstimate(
            flops=count * lines * lanes, bytes_accessed=6 * count * lines * lanes, transcendentals=0
        ),
        name="prefix",
    )(pieces)


def inside_kernel(normed, weight, queries_out, inside_out, table, query_table, sems):
    count, _ = normed.shape
    own_rows, half = queries_out.shape
    heads = half // HD
    fetches = [in_parts(weight.at[0], query_table, sems.at[0], 2)] + [
        in_parts(weight.at[k], table.at[:, pl.ds((k - 1) * half, half)], sems.at[k], 2)
        for k in (1, 2)
    ]
    for some in fetches:
        for fetch in some:
            fetch.start()
    first_row = pl.multiple_of(lax.axis_index("head") * own_rows, own_rows)
    row = lax.broadcasted_iota(jnp.int32, (own_rows, count), 0) + first_row
    causal = row >= lax.broadcasted_iota(jnp.int32, (own_rows, count), 1)
    for fetch in fetches[0]:
        fetch.wait()
    queries = jnp.dot(
        normed[pl.ds(first_row, own_rows), :], query_table[...], preferred_element_type=jnp.float32
    ).astype(jnp.bfloat16)
    queries_out[...] = queries
    for some in fetches[1:]:
        for fetch in some:
            fetch.wait()
    both = jnp.dot(normed[...], table[...], preferred_element_type=jnp.float32)
    both = both.astype(jnp.bfloat16)
    for n in range(heads):
        at = slice(n * HD, (n + 1) * HD)
        scores = lax.dot_general(
            queries[:, at],
            both[:, at],
            (((1,), (1,)), ((), ())),
            preferred_element_type=jnp.float32,
        )
        scores = jnp.where(causal, scores, 0.0).astype(jnp.bfloat16)
        values = both[:, half + n * HD : half + (n + 1) * HD]
        inside_out[:, at] = jnp.dot(scores, values, preferred_element_type=jnp.float32)


def inside_block(normed, weight, own_rows):
    count, width = normed.shape
    half = weight.shape[2]
    local = pl.BlockSpec(memory_space=pltpu.VMEM)
    return pl.pallas_call(
        inside_kernel,
        in_specs=[local, pl.BlockSpec(memory_space=pl.ANY)],
        out_specs=[local] * 2,
        out_shape=[
            pltpu.VMEM((own_rows, half), jnp.bfloat16),
            pltpu.VMEM((own_rows, half), jnp.float32),
        ],
        scratch_shapes=[
            pltpu.VMEM((width, 2 * half), jnp.bfloat16),
            pltpu.VMEM((width, half), jnp.bfloat16),
            pltpu.SemaphoreType.DMA((3, 2)),
        ],
        compiler_params=pltpu.CompilerParams(vmem_limit_bytes=24 * MIB),
        cost_estimate=pl.CostEstimate(
            flops=5 * count * width * half + 4 * own_rows * count * half,
            bytes_accessed=4 * count * width,
            transcendentals=0,
        ),
        name="inside_block",
    )(in_vmem(normed), in_hbm(weight))


def heads_through(queries, inside, state, first, weight):
    own_rows, half = queries.shape
    position = lax.broadcasted_iota(jnp.int32, (own_rows, HD), 0) + first
    unit = 1.0 / (position.astype(jnp.float32) * math.sqrt(HD))
    mixed = []
    for n in range(half // HD):
        at = slice(n * HD, (n + 1) * HD)
        carried = jnp.dot(queries[:, at], state[at, :], preferred_element_type=jnp.float32)
        mixed.append(((inside[:, at] + carried) * unit).astype(jnp.bfloat16))
    return lambda: jnp.dot(
        jnp.concatenate(mixed, axis=1), weight[...], preferred_element_type=jnp.float32
    )


def first_position(own_rows):
    places = lax.axis_index(SEQ) * lax.axis_size("head") + lax.axis_index("head")
    return places * own_rows + 1


def mix_own_kernel(queries, inside, state, out_weight, series, total, weight_in, rows_in, sems):
    own_rows = queries.shape[0]
    first_row = pl.multiple_of(lax.axis_index("head") * own_rows, own_rows)
    fetches = [
        in_parts(out_weight, weight_in, sems.at[0], 2),
        in_parts(series.at[pl.ds(first_row, own_rows)], rows_in, sems.at[1], 2),
    ]
    for some in fetches:
        for fetch in some:
            fetch.start()
    through = heads_through(queries, inside, state, first_position(own_rows), weight_in)
    for some in fetches:
        for fetch in some:
            fetch.wait()
    total[...] = through() + rows_in[...].astype(jnp.float32)


def mix_own(part, state, out_weight, series):
    queries, inside = part
    own_rows, half = queries.shape
    width = series.shape[1]
    anywhere = pl.BlockSpec(memory_space=pl.ANY)
    local = pl.BlockSpec(memory_space=pltpu.VMEM)
    return pl.pallas_call(
        mix_own_kernel,
        in_specs=[local] * 3 + [anywhere] * 2,
        out_specs=local,
        out_shape=pltpu.VMEM((own_rows, width), jnp.float32),
        scratch_shapes=[
            pltpu.VMEM((half, width), jnp.bfloat16),
            pltpu.VMEM((own_rows, width), jnp.bfloat16),
            pltpu.SemaphoreType.DMA((2, 2)),
        ],
        compiler_params=pltpu.CompilerParams(vmem_limit_bytes=16 * MIB),
        cost_estimate=pl.CostEstimate(
            flops=2 * own_rows * half * (width + HD),
            bytes_accessed=8 * own_rows * width,
            transcendentals=0,
        ),
        name="mix_own",
    )(in_vmem(queries), in_vmem(inside), state, in_hbm(out_weight), in_hbm(series))


def mix_kernel(
    queries,
    inside,
    state,
    begun,
    out_weight,
    gain,
    slots,
    ids,
    router,
    slot_column,
    residual_out,
    send_out,
    weight_in,
    router_in,
    sems,
):
    own_rows, width = begun.shape
    fetches = in_parts(out_weight, weight_in, sems.at[0], 2)
    fetch_router = pltpu.make_async_copy(router, router_in, sems.at[1, 0])
    for fetch in fetches:
        fetch.start()
    fetch_router.start()
    slot = lax.broadcasted_iota(jnp.int32, (send_out.shape[0], own_rows), 0)
    chosen = jnp.where(slot == slots[...], 1.0, 0.0).astype(jnp.bfloat16)
    through = heads_through(queries, inside, state, first_position(own_rows), weight_in)
    for fetch in fetches:
        fetch.wait()
    total = begun[...] + through()
    residual_out[:, :width] = total
    normed = normed_rows(total, gain[...]).astype(jnp.bfloat16)
    send_out[...] = jnp.dot(chosen, normed, preferred_element_type=jnp.float32).astype(
        jnp.bfloat16
    )
    fetch_router.wait()
    logits = jnp.dot(normed, router_in[...], preferred_element_type=jnp.float32)
    expert = lax.broadcasted_iota(jnp.int32, logits.shape, 1)
    logit = jnp.sum(jnp.where(expert == ids[...], logits, 0.0), axis=1, keepdims=True)
    residual_out[:, width:] = jnp.broadcast_to(jax.nn.sigmoid(logit), (own_rows, HD))


def mix_heads(part, state, begun, out_weight, gain, slots, ids, router, slot_column, slot_count):
    own_rows, width = begun.shape
    anywhere = pl.BlockSpec(memory_space=pl.ANY)
    local = pl.BlockSpec(memory_space=pltpu.VMEM)
    return pl.pallas_call(
        mix_kernel,
        in_specs=[local] * 4 + [anywhere] + [local] * 3 + [anywhere] * 2,
        out_specs=[local] * 2,
        out_shape=[
            pltpu.VMEM((own_rows, width + HD), jnp.float32),
            jax.ShapeDtypeStruct((slot_count, width), jnp.bfloat16),
        ],
        scratch_shapes=[
            pltpu.VMEM(out_weight.shape, jnp.bfloat16),
            pltpu.VMEM(router.shape, jnp.bfloat16),
            pltpu.SemaphoreType.DMA((2, 2)),
        ],
        compiler_params=pltpu.CompilerParams(vmem_limit_bytes=24 * MIB),
        cost_estimate=pl.CostEstimate(
            flops=2 * own_rows * width * (width + 2 * HD + slot_count),
            bytes_accessed=12 * own_rows * width,
            transcendentals=own_rows,
        ),
        name="mix_heads",
    )(
        *(in_vmem(array) for array in part),
        state,
        in_vmem(begun),
        in_hbm(out_weight),
        gain,
        slots,
        ids,
        in_hbm(router),
        slot_column,
    )


def combine_kernel(returned, residual, slots, out, held, sems):
    own_rows, width = held.shape
    parts = 4
    leave = in_parts(held, out, sems, parts)
    slot = lax.broadcasted_iota(jnp.int32, (own_rows, returned.shape[0]), 1)
    chosen = jnp.where(slot == slots[...], 1.0, 0.0).astype(jnp.bfloat16)
    size = own_rows // parts
    for k in range(parts):
        at = slice(k * size, (k + 1) * size)
        routed = jnp.dot(chosen[at], returned[...], preferred_element_type=jnp.float32)
        weight = jnp.concatenate([residual[at, width:]] * (width // HD), axis=1)
        held[at, :] = (residual[at, :width] + weight * routed).astype(jnp.bfloat16)
        leave[k].start()
    for copy in leave:
        copy.wait()


def combine(returned, residual, slots):
    own_rows, width = residual.shape[0], returned.shape[1]
    anywhere = pl.BlockSpec(memory_space=pl.ANY)
    local = pl.BlockSpec(memory_space=pltpu.VMEM)
    return pl.pallas_call(
        combine_kernel,
        in_specs=[local] * 3,
        out_specs=anywhere,
        out_shape=pltpu.HBM((own_rows, width), jnp.bfloat16),
        scratch_shapes=[
            pltpu.VMEM((own_rows, width), jnp.bfloat16),
            pltpu.SemaphoreType.DMA((4,)),
        ],
        compiler_params=pltpu.CompilerParams(vmem_limit_bytes=24 * MIB),
        cost_estimate=pl.CostEstimate(
            flops=2 * own_rows * width * returned.shape[0],
            bytes_accessed=10 * own_rows * width,
            transcendentals=0,
        ),
        name="combine",
    )(returned, in_vmem(residual), slots)


def on_device(
    series,
    norm_attn,
    qkv_weight,
    out_weight,
    norm_moe,
    router_weight,
    expert_ids,
    gate_weight,
    up_weight,
    down_weight,
):
    width = series.shape[2]
    head_count = lax.axis_size("head")
    seq_size = lax.axis_size(SEQ)
    own_rows = series.shape[1] // head_count

    qkv_own = jnp.moveaxis(qkv_weight, 1, 0)
    own_expert = (gate_weight[0], up_weight[0], down_weight[0])
    qkv_other = from_partner(qkv_own)
    out_other = from_partner(out_weight)
    gate_other, up_other = (from_partner(w) for w in own_expert[:2])
    down_other = from_partner(own_expert[2])
    other_expert = (gate_other, up_other, down_other)

    state, normed_in = block_state(series[0], qkv_own, norm_attn)
    pieces = exchange(state.reshape(seq_size, state.shape[0] // seq_size, HD), SEQ)
    state_own = exchange(prefix(pieces), SEQ)
    state_other = from_partner(state_own)
    part_own = inside_block(normed_in, qkv_own, own_rows)
    part_other = inside_block(normed_in, qkv_other, own_rows)

    route_ids = expert_ids[0, :, 0]
    expert_count = router_weight.shape[1]
    capacity = 2 * own_rows // expert_count
    earlier_row = jnp.arange(own_rows)[None, :] < jnp.arange(own_rows)[:, None]
    same_expert = route_ids[:, None] == route_ids[None, :]
    slot_rank = jnp.sum(jnp.logical_and(same_expert, earlier_row), axis=1)
    slot_index = route_ids * capacity + slot_rank
    slots = slot_index[None, :]
    slot_column = slot_index[:, None]

    begun = mix_own(part_own, state_own.reshape(state.shape), out_weight, series[0])
    residual, send_buffer = mix_heads(
        part_other,
        state_other.reshape(state.shape),
        begun,
        out_other,
        norm_moe,
        slots,
        route_ids[:, None],
        router_weight,
        slot_column,
        expert_count * capacity,
    )
    received = exchange(send_buffer.reshape(expert_count, capacity, width), SEQ_DP)

    expert_out = expert_of(received.reshape(-1, width), own_expert, other_expert)
    returned = exchange(expert_out.reshape(received.shape), SEQ_DP)
    layer_out = combine(returned.reshape(send_buffer.shape), residual, slot_column)
    return layer_out[None]


def solution(mesh):
    split = Mesh(
        mesh.devices.reshape(8, 4, mesh.shape["head"], mesh.shape["dp"]),
        ("seq_0", "seq_1", "head", "dp"),
    )
    placed = (
        P("dp", SEQ, None),
        P(),
        P(None, None, "head"),
        P("head", None),
        P(),
        P(),
        P("dp", SEQ_HEAD, None),
        P(SEQ_DP, None, "head"),
        P(SEQ_DP, None, "head"),
        P(SEQ_DP, "head", None),
    )

    return jax.shard_map(
        on_device, mesh=split, in_specs=placed, out_specs=P("dp", SEQ_HEAD, None), check_vma=False
    )
```

profile of v0, /device:TPU:32, one launch (start us, length us, event | category | flops | bytes accessed | tf_op | source)
XLA Modules:
  0.0 129.4 jit_solution(14654407994810016531)
XLA Ops:
  0.0 0.0 copy-start.1
  0.0 0.0 copy-start.3
  0.0 0.0 collective-permute-start
  0.0 3.6 %block_state.1 = (bf16[512,128]{1,0:T(8,128)(2,1)}, bf16[512,768]{1,0:T(8,128)(2,1)S(1)}) custom-call(bf16[512,768]{1,0:T(8,128)(2,1)} %bitcast.17, bf16[3,768,384]{2,1,0:T(8,128)(2,1)} %bitcast.20, f32[768]{0:T(1024)} %gain.2), custom_call_target="tpu_custom_call" | custom-call | flops 603979776 | bytes 1572864 | tf_op jit(solution)/shard_map/block_state/pallas_call | solution.py:166
  3.6 11.4 %all-to-all-start = ((bf16[32,16,128]{2,1,0:T(8,128)(2,1)}), bf16[32,16,128]{2,1,0:T(8,128)(2,1)S(1)}, u32[]{:S(2)}, u32[]{:S(2)}) async-start(bf16[32,16,128]{2,1,0:T(8,128)(2,1)} %bitcast.2), calls=%async_computation | async-start | bytes 262144 | tf_op jit(solution)/shard_map/all_to_all | solution.py:26
  15.0 0.0 copy-done.1
  15.0 0.1 collective-permute-start.2
  15.1 0.5 collective-permute-start.3
  15.6 0.1 collective-permute-start.4
  15.7 0.4 collective-permute-start.5
  16.1 0.0 copy-done.3
  16.1 0.2 convert_reduce_fusion
  16.3 8.9 %all-to-all-done.pieces = bf16[32,16,128]{2,1,0:T(8,128)(2,1)S(1)} async-done(((bf16[32,16,128]{2,1,0:T(8,128)(2,1)}), bf16[32,16,128]{2,1,0:T(8,128)(2,1)S(1)}, u32[]{:S(2)}, u32[]{:S(2)}) %all-to-all-start) | async-done | bytes 131104 | tf_op jit(solution)/shard_map/all_to_all | solution.py:26
  25.2 0.7 prefix.1
  25.9 4.6 %all-to-all-start.1 = ((bf16[32,16,128]{2,1,0:T(8,128)(2,1)}), bf16[32,16,128]{2,1,0:T(8,128)(2,1)S(1)}, u32[]{:S(2)}, u32[]{:S(2)}) async-start(bf16[32,16,128]{2,1,0:T(8,128)(2,1)} %prefix.1), calls=%async_computation.1 | async-start | bytes 262144 | tf_op jit(solution)/shard_map/all_to_all | solution.py:26
  30.4 0.1 copy.20.ids
  30.6 0.1 copy.19
  30.8 9.3 %all-to-all-done.1 = bf16[32,16,128]{2,1,0:T(8,128)(2,1)S(1)} async-done(((bf16[32,16,128]{2,1,0:T(8,128)(2,1)}), bf16[32,16,128]{2,1,0:T(8,128)(2,1)S(1)}, u32[]{:S(2)}, u32[]{:S(2)}) %all-to-all-start.1) | async-done | bytes 131104 | tf_op jit(solution)/shard_map/all_to_all | solution.py:26
  40.1 0.0 collective-permute-done.weight
  40.1 0.0 collective-permute-start.1
  40.1 2.8 %inside_block.3 = (bf16[256,384]{1,0:T(8,128)(2,1)S(1)}, f32[256,384]{1,0:T(8,128)S(1)}) custom-call(bf16[512,768]{1,0:T(8,128)(2,1)S(1)} %get-tuple-element.13.normed, bf16[3,768,384]{2,1,0:T(8,128)(2,1)} %bitcast.21), custom_call_target="tpu_custom_call" | custom-call | flops 956301312 | bytes 1572864 | tf_op jit(solution)/shard_map/inside_block/pallas_call | solution.py:257
  42.9 1.6 %mix_own.1.begun = f32[256,768]{1,0:T(8,128)S(1)} custom-call(bf16[256,384]{1,0:T(8,128)(2,1)S(1)} %get-tuple-element.17.queries, f32[256,384]{1,0:T(8,128)S(1)} %get-tuple-element.18.inside, bf16[512,128]{1,0:T(8,128)(2,1)S(1)} %bitcast.15, bf16[384,768]{1,0:T(8,128)(2,1)} %out_weight.1, bf16[512,768]{1,0:T(8,128)(2,1)} %bitcast.18), custom_call_target="tpu_custom_call" | custom-call | flops 176160768 | bytes 1572864 | tf_op jit(solution)/shard_map/mix_own/pallas_call | solution.py:322
  44.5 0.0 copy-start
  44.5 2.8 %inside_block.2 = (bf16[256,384]{1,0:T(8,128)(2,1)S(1)}, f32[256,384]{1,0:T(8,128)S(1)}) custom-call(bf16[512,768]{1,0:T(8,128)(2,1)S(1)} %get-tuple-element.13.normed, bf16[3,768,384]{2,1,0:T(8,128)(2,1)} %collective-permute-done.weight), custom_call_target="tpu_custom_call" | custom-call | flops 956301312 | bytes 1572864 | tf_op jit(solution)/shard_map/inside_block/pallas_call | solution.py:257
  47.4 0.0 collective-permute-done.2.out_weight
  47.4 0.0 copy-start.2
  47.4 0.0 collective-permute-done.1
  47.4 0.8 copy-done.2
  48.2 0.0 copy-done
  48.2 2.5 %mix_heads.1 = (f32[256,896]{1,0:T(8,128)S(1)}, bf16[512,768]{1,0:T(8,128)(2,1)S(1)}) custom-call(bf16[256,384]{1,0:T(8,128)(2,1)S(1)} %get-tuple-element.14.queries, f32[256,384]{1,0:T(8,128)S(1)} %get-tuple-element.15.inside, bf16[512,128]{1,0:T(8,128)(2,1)S(1)} %bitcast.16, f32[256,768]{1,0:T(8,128)S(1)} %mix_own.1.begun, bf16[384,768]{1,0:T(8,128)(2,1)} %copy-done.2, ...), custom_call_target="tpu_custom_call" | custom-call | flops 603979776 | bytes 2359296 | tf_op jit(solution)/shard_map/mix_heads/pallas_call | solution.py:387
  50.7 0.2 reshape.62
  50.9 34.4 %all_to_all.20 = bf16[128,4,768]{2,1,0:T(4,128)(2,1)S(1)} all-to-all(bf16[128,4,768]{2,1,0:T(4,128)(2,1)S(1)} %reshape.62), channel_id=1, replica_groups=mesh['seq_0'=8,'seq_1'=4,'head'=2,'dp'=4] {'seq_0','seq_1','dp'}, dimensions={0} | all-to-all | bytes 1572864 | tf_op jit(solution)/shard_map/all_to_all | solution.py:26
  85.3 0.2 reshape.63.rows
  85.5 0.0 collective-permute-done.3.gate_b
  85.5 0.0 collective-permute-done.4.up_b
  85.5 0.0 collective-permute-done.5.down_b
  85.5 10.9 %expert_mlp.1 = bf16[512,768]{1,0:T(8,128)(2,1)S(1)} custom-call(bf16[512,768]{1,0:T(8,128)(2,1)S(1)} %reshape.63.rows, bf16[768,1536]{1,0:T(8,128)(2,1)} %bitcast.27, bf16[768,1536]{1,0:T(8,128)(2,1)} %bitcast.29, bf16[1536,768]{1,0:T(8,128)(2,1)} %bitcast.31, bf16[768,1536]{1,0:T(8,128)(2,1)} %collective-permute-done.3.gate_b, ...), custom_call_target="tpu_custom_call" | custom-call | flops 7247757312 | bytes 14155776 | tf_op jit(solution)/shard_map/expert_mlp/pallas_call | solution.py:81
  96.5 0.2 reshape.64
  96.7 31.0 %all_to_all.21 = bf16[128,4,768]{2,1,0:T(4,128)(2,1)S(1)} all-to-all(bf16[128,4,768]{2,1,0:T(4,128)(2,1)S(1)} %reshape.64), channel_id=1, replica_groups=mesh['seq_0'=8,'seq_1'=4,'head'=2,'dp'=4] {'seq_0','seq_1','dp'}, dimensions={0} | all-to-all | bytes 1572864 | tf_op jit(solution)/shard_map/all_to_all | solution.py:26
  127.7 0.2 reshape.65.returned
  127.9 1.4 %combine.1 = bf16[256,768]{1,0:T(8,128)(2,1)} custom-call(bf16[512,768]{1,0:T(8,128)(2,1)S(1)} %reshape.65.returned, f32[256,896]{1,0:T(8,128)S(1)} %get-tuple-element.20.residual, s32[256,1]{1,0:T(8,128)S(1)} %multiply_add_fusion.slot_column.slots), custom_call_target="tpu_custom_call" | custom-call | flops 201326592 | bytes 1966080 | tf_op jit(solution)/shard_map/combine/pallas_call | solution.py:441
  (2 shorter events, 0.0 us)
Async XLA Ops:
  0.0 15.0 %copy-start.1 = (bf16[384,768]{1,0:T(8,128)(2,1)S(1)}, bf16[384,768]{1,0:T(8,128)(2,1)}, u32[]{:S(2)}) copy-start(bf16[384,768]{1,0:T(8,128)(2,1)} %out_weight.1) | copy-start | bytes 1769476
  0.0 16.1 %copy-start.3 = (s32[1,256,1]{1,2,0:T(1,128)S(1)}, s32[1,256,1]{1,2,0:T(1,128)}, u32[]{:S(2)}) copy-start(s32[1,256,1]{1,2,0:T(1,128)} %param.16) | copy-start | bytes 3076
  0.0 40.1 %collective-permute-start = (bf16[3,768,384]{2,1,0:T(8,128)(2,1)}, bf16[3,768,384]{2,1,0:T(8,128)(2,1)}, u32[]{:S(2)}, u32[]{:S(2)}) collective-permute-start(bf16[3,768,384]{2,1,0:T(8,128)(2,1)} %bitcast.19), channel_id=1, source_target_pairs={{0,4},{4,0},{1,5},{5,1},{2,6},{6,2},{3,7},{7,3},{8,12},{12,8},{9,1... | collective-permute-start | bytes 5308424 | tf_op jit(solution)/shard_map/ppermute | solution.py:22
  3.6 21.6 %all-to-all-start = ((bf16[32,16,128]{2,1,0:T(8,128)(2,1)}), bf16[32,16,128]{2,1,0:T(8,128)(2,1)S(1)}, u32[]{:S(2)}, u32[]{:S(2)}) async-start(bf16[32,16,128]{2,1,0:T(8,128)(2,1)} %bitcast.2), calls=%async_computation | async-start | bytes 262144 | tf_op jit(solution)/shard_map/all_to_all | solution.py:26
  15.0 32.4 %collective-permute-start.2 = (bf16[384,768]{1,0:T(8,128)(2,1)S(1)}, bf16[384,768]{1,0:T(8,128)(2,1)S(1)}, u32[]{:S(2)}, u32[]{:S(2)}) collective-permute-start(bf16[384,768]{1,0:T(8,128)(2,1)S(1)} %copy-done.1), channel_id=1, source_target_pairs={{0,4},{4,0},{1,5},{5,1},{2,6},{6,2},{3,7},{7,3},{8,12},{12,8},{9,1... | collective-permute-start | bytes 1769480 | tf_op jit(solution)/shard_map/ppermute | solution.py:22
  15.1 70.4 %collective-permute-start.3 = (bf16[768,1536]{1,0:T(8,128)(2,1)}, bf16[768,1536]{1,0:T(8,128)(2,1)}, u32[]{:S(2)}, u32[]{:S(2)}) collective-permute-start(bf16[768,1536]{1,0:T(8,128)(2,1)} %bitcast.26), channel_id=1, source_target_pairs={{0,4},{4,0},{1,5},{5,1},{2,6},{6,2},{3,7},{7,3},{8,12},{12,8},{9,1... | collective-permute-start | bytes 7077896 | tf_op jit(solution)/shard_map/ppermute | solution.py:22
  15.6 69.9 %collective-permute-start.4 = (bf16[768,1536]{1,0:T(8,128)(2,1)}, bf16[768,1536]{1,0:T(8,128)(2,1)}, u32[]{:S(2)}, u32[]{:S(2)}) collective-permute-start(bf16[768,1536]{1,0:T(8,128)(2,1)} %bitcast.28), channel_id=1, source_target_pairs={{0,4},{4,0},{1,5},{5,1},{2,6},{6,2},{3,7},{7,3},{8,12},{12,8},{9,1... | collective-permute-start | bytes 7077896 | tf_op jit(solution)/shard_map/ppermute | solution.py:22
  15.7 69.9 %collective-permute-start.5 = (bf16[1536,768]{1,0:T(8,128)(2,1)}, bf16[1536,768]{1,0:T(8,128)(2,1)}, u32[]{:S(2)}, u32[]{:S(2)}) collective-permute-start(bf16[1536,768]{1,0:T(8,128)(2,1)} %bitcast.30), channel_id=1, source_target_pairs={{0,4},{4,0},{1,5},{5,1},{2,6},{6,2},{3,7},{7,3},{8,12},{12,8},{9,1... | collective-permute-start | bytes 7077896 | tf_op jit(solution)/shard_map/ppermute | solution.py:22
  25.9 14.2 %all-to-all-start.1 = ((bf16[32,16,128]{2,1,0:T(8,128)(2,1)}), bf16[32,16,128]{2,1,0:T(8,128)(2,1)S(1)}, u32[]{:S(2)}, u32[]{:S(2)}) async-start(bf16[32,16,128]{2,1,0:T(8,128)(2,1)} %prefix.1), calls=%async_computation.1 | async-start | bytes 262144 | tf_op jit(solution)/shard_map/all_to_all | solution.py:26
  40.1 7.3 %collective-permute-start.1 = (bf16[32,16,128]{2,1,0:T(8,128)(2,1)S(1)}, bf16[32,16,128]{2,1,0:T(8,128)(2,1)S(1)}, u32[]{:S(2)}, u32[]{:S(2)}) collective-permute-start(bf16[32,16,128]{2,1,0:T(8,128)(2,1)S(1)} %all-to-all-done.1), channel_id=1, source_target_pairs={{0,4},{4,0},{1,5},{5,1},{2,6},{6,2},{3,7},{7,3},{8,12},{12,8},{9,1... | collective-permute-start | bytes 393224 | tf_op jit(solution)/shard_map/ppermute | solution.py:22
  44.5 3.7 %copy-start = (f32[768]{0:T(1024)S(1)}, f32[768]{0:T(1024)}, u32[]{:S(2)}) copy-start(f32[768]{0:T(1024)} %gain.3) | copy-start | bytes 9220
  47.4 0.8 copy-start.2
where the time goes:
time: 130 us; the launch traced here: 129 us
  blocking collectives  65.5 us (50%)
  Pallas kernels  26.3 us (20%)
  waiting for transfers between devices  18.2 us (14%)
  starting transfers between devices  17 us (13%)
  local copies, waits for them, and re-layouts  1.79 us (1%)
    all_to_all x2, blocking collectives, exchange(): return lax.all_to_all(pieces, axes, split_axis=0, concat_axis=0, tiled=True)  65.5 us
    all_to_all x2, waiting for transfers between devices, exchange(): return lax.all_to_all(pieces, axes, split_axis=0, concat_axis=0, tiled=True)  18.2 us
    all_to_all x2, starting transfers between devices, exchange(): return lax.all_to_all(pieces, axes, split_axis=0, concat_axis=0, tiled=True)  15.9 us
    pallas_call x1, Pallas kernels, expert_of(): pl.pallas_call(expert_kernel, in_specs=[local] + [pl.BlockSpec(memory_spa...  10.9 us
    pallas_call x2, Pallas kernels, inside_block(): pl.pallas_call(inside_kernel, in_specs=[local, pl.BlockSpec(memory_space=...  5.66 us
    pallas_call x1, Pallas kernels, block_state(): pl.pallas_call(state_kernel, in_specs=[pl.BlockSpec(memory_space=pl.ANY),...  3.56 us
  transfers between devices with their start and end apart: 8, of which 2 were waited for; matrix products, arithmetic and copies ran while one was open for 1% of the time, Pallas kernels for 11%

commit v1 on v0

--- a/solution.py
+++ b/solution.py
@@ -14,7 +14,8 @@
 SEQ_DP = ("seq_0", "seq_1", "dp")
 SEQ_HEAD = ("seq_0", "seq_1", "head")
 NORM_EPS = 1e-06
-FF_BLOCK = 512
+FF_BLOCK = 1536
+FF_FIRST = 512
 MIB = 1024 * 1024
 
 
@@ -29,12 +30,12 @@
 def expert_kernel(rows, gate_a, up_a, down_a, gate_b, up_b, down_b, out, gate, up, down, total, sems):
     blocks = gate.shape[0]
     own_blocks = blocks // 2
-    first = FF_BLOCK // 2
+    first = FF_FIRST
 
     def copies(k):
         gates, ups, downs = (gate_a, up_a, down_a) if k < own_blocks else (gate_b, up_b, down_b)
         base = (k % own_blocks) * FF_BLOCK
-        spans = ((0, first), (first, first)) if k == 0 else ((0, FF_BLOCK),)
+        spans = ((0, first), (first, FF_BLOCK - first)) if k == 0 else ((0, FF_BLOCK),)
         for n, (at, size) in enumerate(spans):
             row = 0 if k == 0 and n == 0 else k + 1
             to, source = pl.ds(at, size), pl.ds(base + at, size)
@@ -478,9 +479,7 @@
     own_expert = (gate_weight[0], up_weight[0], down_weight[0])
     qkv_other = from_partner(qkv_own)
     out_other = from_partner(out_weight)
-    gate_other, up_other = (from_partner(w) for w in own_expert[:2])
-    down_other = from_partner(own_expert[2])
-    other_expert = (gate_other, up_other, down_other)
+    other_expert = tuple(from_partner(w) for w in own_expert)
 
     state, normed_in = block_state(series[0], qkv_own, norm_attn)
     pieces = exchange(state.reshape(seq_size, state.shape[0] // seq_size, HD), SEQ)

time: 130 us -> 129 us (level)
  no operation moved by 1% of the time
where the time goes in v1:
time: 129 us
  blocking collectives  65.5 us (51%)
  Pallas kernels  25.8 us (20%)
  waiting for transfers between devices  18.2 us (14%)
  starting transfers between devices  17 us (13%)
  local copies, waits for them, and re-layouts  1.79 us (1%)
    all_to_all x2, blocking collectives, exchange(): return lax.all_to_all(pieces, axes, split_axis=0, concat_axis=0, tiled=True)  65.5 us
    all_to_all x2, waiting for transfers between devices, exchange(): return lax.all_to_all(pieces, axes, split_axis=0, concat_axis=0, tiled=True)  18.2 us
    all_to_all x2, starting transfers between devices, exchange(): return lax.all_to_all(pieces, axes, split_axis=0, concat_axis=0, tiled=True)  15.9 us
    pallas_call x1, Pallas kernels, expert_of(): pl.pallas_call(expert_kernel, in_specs=[local] + [pl.BlockSpec(memory_spa...  10.4 us
    pallas_call x2, Pallas kernels, inside_block(): pl.pallas_call(inside_kernel, in_specs=[local, pl.BlockSpec(memory_space=...  5.66 us
    pallas_call x1, Pallas kernels, block_state(): pl.pallas_call(state_kernel, in_specs=[pl.BlockSpec(memory_space=pl.ANY),...  3.56 us
  transfers between devices with their start and end apart: 8, of which 2 were waited for; matrix products, arithmetic and copies ran while one was open for 1% of the time, Pallas kernels for 11%

profile of v1, /device:TPU:32, one launch (start us, length us, event | category | flops | bytes accessed | tf_op | source)
XLA Modules:
  0.0 128.9 jit_solution(12648215423546546292)
XLA Ops:
  0.0 0.0 copy-start.1
  0.0 0.0 copy-start.3
  0.0 0.0 collective-permute-start
  0.0 3.6 %block_state.1 = (bf16[512,128]{1,0:T(8,128)(2,1)}, bf16[512,768]{1,0:T(8,128)(2,1)S(1)}) custom-call(bf16[512,768]{1,0:T(8,128)(2,1)} %bitcast.17, bf16[3,768,384]{2,1,0:T(8,128)(2,1)} %bitcast.20, f32[768]{0:T(1024)} %gain.2), custom_call_target="tpu_custom_call" | custom-call | flops 603979776 | bytes 1572864 | tf_op jit(solution)/shard_map/block_state/pallas_call | solution.py:167
  3.6 11.4 %all-to-all-start = ((bf16[32,16,128]{2,1,0:T(8,128)(2,1)}), bf16[32,16,128]{2,1,0:T(8,128)(2,1)S(1)}, u32[]{:S(2)}, u32[]{:S(2)}) async-start(bf16[32,16,128]{2,1,0:T(8,128)(2,1)} %bitcast.2), calls=%async_computation | async-start | bytes 262144 | tf_op jit(solution)/shard_map/all_to_all | solution.py:27
  15.0 0.0 copy-done.1
  15.0 0.1 collective-permute-start.2
  15.1 0.5 collective-permute-start.3
  15.6 0.1 collective-permute-start.4
  15.7 0.4 collective-permute-start.5
  16.1 0.0 copy-done.3
  16.1 0.2 convert_reduce_fusion
  16.3 8.9 %all-to-all-done.pieces = bf16[32,16,128]{2,1,0:T(8,128)(2,1)S(1)} async-done(((bf16[32,16,128]{2,1,0:T(8,128)(2,1)}), bf16[32,16,128]{2,1,0:T(8,128)(2,1)S(1)}, u32[]{:S(2)}, u32[]{:S(2)}) %all-to-all-start) | async-done | bytes 131104 | tf_op jit(solution)/shard_map/all_to_all | solution.py:27
  25.2 0.7 prefix.1
  25.9 4.6 %all-to-all-start.1 = ((bf16[32,16,128]{2,1,0:T(8,128)(2,1)}), bf16[32,16,128]{2,1,0:T(8,128)(2,1)S(1)}, u32[]{:S(2)}, u32[]{:S(2)}) async-start(bf16[32,16,128]{2,1,0:T(8,128)(2,1)} %prefix.1), calls=%async_computation.1 | async-start | bytes 262144 | tf_op jit(solution)/shard_map/all_to_all | solution.py:27
  30.4 0.1 copy.20.ids
  30.6 0.1 copy.19
  30.8 9.3 %all-to-all-done.1 = bf16[32,16,128]{2,1,0:T(8,128)(2,1)S(1)} async-done(((bf16[32,16,128]{2,1,0:T(8,128)(2,1)}), bf16[32,16,128]{2,1,0:T(8,128)(2,1)S(1)}, u32[]{:S(2)}, u32[]{:S(2)}) %all-to-all-start.1) | async-done | bytes 131104 | tf_op jit(solution)/shard_map/all_to_all | solution.py:27
  40.1 0.0 collective-permute-done.weight
  40.1 0.0 collective-permute-start.1
  40.1 2.8 %inside_block.3 = (bf16[256,384]{1,0:T(8,128)(2,1)S(1)}, f32[256,384]{1,0:T(8,128)S(1)}) custom-call(bf16[512,768]{1,0:T(8,128)(2,1)S(1)} %get-tuple-element.13.normed, bf16[3,768,384]{2,1,0:T(8,128)(2,1)} %bitcast.21), custom_call_target="tpu_custom_call" | custom-call | flops 956301312 | bytes 1572864 | tf_op jit(solution)/shard_map/inside_block/pallas_call | solution.py:258
  42.9 1.6 %mix_own.1.begun = f32[256,768]{1,0:T(8,128)S(1)} custom-call(bf16[256,384]{1,0:T(8,128)(2,1)S(1)} %get-tuple-element.17.queries, f32[256,384]{1,0:T(8,128)S(1)} %get-tuple-element.18.inside, bf16[512,128]{1,0:T(8,128)(2,1)S(1)} %bitcast.15, bf16[384,768]{1,0:T(8,128)(2,1)} %out_weight.1, bf16[512,768]{1,0:T(8,128)(2,1)} %bitcast.18), custom_call_target="tpu_custom_call" | custom-call | flops 176160768 | bytes 1572864 | tf_op jit(solution)/shard_map/mix_own/pallas_call | solution.py:323
  44.5 0.0 copy-start
  44.5 2.8 %inside_block.2 = (bf16[256,384]{1,0:T(8,128)(2,1)S(1)}, f32[256,384]{1,0:T(8,128)S(1)}) custom-call(bf16[512,768]{1,0:T(8,128)(2,1)S(1)} %get-tuple-element.13.normed, bf16[3,768,384]{2,1,0:T(8,128)(2,1)} %collective-permute-done.weight), custom_call_target="tpu_custom_call" | custom-call | flops 956301312 | bytes 1572864 | tf_op jit(solution)/shard_map/inside_block/pallas_call | solution.py:258
  47.4 0.0 collective-permute-done.2.out_weight
  47.4 0.0 copy-start.2
  47.4 0.0 collective-permute-done.1
  47.4 0.8 copy-done.2
  48.2 0.0 copy-done
  48.2 2.5 %mix_heads.1 = (f32[256,896]{1,0:T(8,128)S(1)}, bf16[512,768]{1,0:T(8,128)(2,1)S(1)}) custom-call(bf16[256,384]{1,0:T(8,128)(2,1)S(1)} %get-tuple-element.14.queries, f32[256,384]{1,0:T(8,128)S(1)} %get-tuple-element.15.inside, bf16[512,128]{1,0:T(8,128)(2,1)S(1)} %bitcast.16, f32[256,768]{1,0:T(8,128)S(1)} %mix_own.1.begun, bf16[384,768]{1,0:T(8,128)(2,1)} %copy-done.2, ...), custom_call_target="tpu_custom_call" | custom-call | flops 603979776 | bytes 2359296 | tf_op jit(solution)/shard_map/mix_heads/pallas_call | solution.py:388
  50.7 0.2 reshape.62
  50.9 34.4 %all_to_all.20 = bf16[128,4,768]{2,1,0:T(4,128)(2,1)S(1)} all-to-all(bf16[128,4,768]{2,1,0:T(4,128)(2,1)S(1)} %reshape.62), channel_id=1, replica_groups=mesh['seq_0'=8,'seq_1'=4,'head'=2,'dp'=4] {'seq_0','seq_1','dp'}, dimensions={0} | all-to-all | bytes 1572864 | tf_op jit(solution)/shard_map/all_to_all | solution.py:27
  85.3 0.2 reshape.63.rows
  85.5 0.0 collective-permute-done.3.gate_b
  85.5 0.0 collective-permute-done.4.up_b
  85.5 0.0 collective-permute-done.5.down_b
  85.5 10.4 %expert_mlp.1 = bf16[512,768]{1,0:T(8,128)(2,1)S(1)} custom-call(bf16[512,768]{1,0:T(8,128)(2,1)S(1)} %reshape.63.rows, bf16[768,1536]{1,0:T(8,128)(2,1)} %bitcast.27, bf16[768,1536]{1,0:T(8,128)(2,1)} %bitcast.29, bf16[1536,768]{1,0:T(8,128)(2,1)} %bitcast.31, bf16[768,1536]{1,0:T(8,128)(2,1)} %collective-permute-done.3.gate_b, ...), custom_call_target="tpu_custom_call" | custom-call | flops 7247757312 | bytes 14155776 | tf_op jit(solution)/shard_map/expert_mlp/pallas_call | solution.py:82
  95.9 0.2 reshape.64
  96.1 31.0 %all_to_all.21 = bf16[128,4,768]{2,1,0:T(4,128)(2,1)S(1)} all-to-all(bf16[128,4,768]{2,1,0:T(4,128)(2,1)S(1)} %reshape.64), channel_id=1, replica_groups=mesh['seq_0'=8,'seq_1'=4,'head'=2,'dp'=4] {'seq_0','seq_1','dp'}, dimensions={0} | all-to-all | bytes 1572864 | tf_op jit(solution)/shard_map/all_to_all | solution.py:27
  127.1 0.2 reshape.65.returned
  127.3 1.4 %combine.1 = bf16[256,768]{1,0:T(8,128)(2,1)} custom-call(bf16[512,768]{1,0:T(8,128)(2,1)S(1)} %reshape.65.returned, f32[256,896]{1,0:T(8,128)S(1)} %get-tuple-element.20.residual, s32[256,1]{1,0:T(8,128)S(1)} %multiply_add_fusion.slot_column.slots), custom_call_target="tpu_custom_call" | custom-call | flops 201326592 | bytes 1966080 | tf_op jit(solution)/shard_map/combine/pallas_call | solution.py:442
  (2 shorter events, 0.0 us)
Async XLA Ops:
  0.0 15.0 %copy-start.1 = (bf16[384,768]{1,0:T(8,128)(2,1)S(1)}, bf16[384,768]{1,0:T(8,128)(2,1)}, u32[]{:S(2)}) copy-start(bf16[384,768]{1,0:T(8,128)(2,1)} %out_weight.1) | copy-start | bytes 1769476
  0.0 16.1 %copy-start.3 = (s32[1,256,1]{1,2,0:T(1,128)S(1)}, s32[1,256,1]{1,2,0:T(1,128)}, u32[]{:S(2)}) copy-start(s32[1,256,1]{1,2,0:T(1,128)} %param.16) | copy-start | bytes 3076
  0.0 40.1 %collective-permute-start = (bf16[3,768,384]{2,1,0:T(8,128)(2,1)}, bf16[3,768,384]{2,1,0:T(8,128)(2,1)}, u32[]{:S(2)}, u32[]{:S(2)}) collective-permute-start(bf16[3,768,384]{2,1,0:T(8,128)(2,1)} %bitcast.19), channel_id=1, source_target_pairs={{0,4},{4,0},{1,5},{5,1},{2,6},{6,2},{3,7},{7,3},{8,12},{12,8},{9,1... | collective-permute-start | bytes 5308424 | tf_op jit(solution)/shard_map/ppermute | solution.py:23
  3.6 21.6 %all-to-all-start = ((bf16[32,16,128]{2,1,0:T(8,128)(2,1)}), bf16[32,16,128]{2,1,0:T(8,128)(2,1)S(1)}, u32[]{:S(2)}, u32[]{:S(2)}) async-start(bf16[32,16,128]{2,1,0:T(8,128)(2,1)} %bitcast.2), calls=%async_computation | async-start | bytes 262144 | tf_op jit(solution)/shard_map/all_to_all | solution.py:27
  15.0 32.4 %collective-permute-start.2 = (bf16[384,768]{1,0:T(8,128)(2,1)S(1)}, bf16[384,768]{1,0:T(8,128)(2,1)S(1)}, u32[]{:S(2)}, u32[]{:S(2)}) collective-permute-start(bf16[384,768]{1,0:T(8,128)(2,1)S(1)} %copy-done.1), channel_id=1, source_target_pairs={{0,4},{4,0},{1,5},{5,1},{2,6},{6,2},{3,7},{7,3},{8,12},{12,8},{9,1... | collective-permute-start | bytes 1769480 | tf_op jit(solution)/shard_map/ppermute | solution.py:23
  15.1 70.4 %collective-permute-start.3 = (bf16[768,1536]{1,0:T(8,128)(2,1)}, bf16[768,1536]{1,0:T(8,128)(2,1)}, u32[]{:S(2)}, u32[]{:S(2)}) collective-permute-start(bf16[768,1536]{1,0:T(8,128)(2,1)} %bitcast.26), channel_id=1, source_target_pairs={{0,4},{4,0},{1,5},{5,1},{2,6},{6,2},{3,7},{7,3},{8,12},{12,8},{9,1... | collective-permute-start | bytes 7077896 | tf_op jit(solution)/shard_map/ppermute | solution.py:23
  15.6 69.9 %collective-permute-start.4 = (bf16[768,1536]{1,0:T(8,128)(2,1)}, bf16[768,1536]{1,0:T(8,128)(2,1)}, u32[]{:S(2)}, u32[]{:S(2)}) collective-permute-start(bf16[768,1536]{1,0:T(8,128)(2,1)} %bitcast.28), channel_id=1, source_target_pairs={{0,4},{4,0},{1,5},{5,1},{2,6},{6,2},{3,7},{7,3},{8,12},{12,8},{9,1... | collective-permute-start | bytes 7077896 | tf_op jit(solution)/shard_map/ppermute | solution.py:23
  15.7 69.9 %collective-permute-start.5 = (bf16[1536,768]{1,0:T(8,128)(2,1)}, bf16[1536,768]{1,0:T(8,128)(2,1)}, u32[]{:S(2)}, u32[]{:S(2)}) collective-permute-start(bf16[1536,768]{1,0:T(8,128)(2,1)} %bitcast.30), channel_id=1, source_target_pairs={{0,4},{4,0},{1,5},{5,1},{2,6},{6,2},{3,7},{7,3},{8,12},{12,8},{9,1... | collective-permute-start | bytes 7077896 | tf_op jit(solution)/shard_map/ppermute | solution.py:23
  25.9 14.2 %all-to-all-start.1 = ((bf16[32,16,128]{2,1,0:T(8,128)(2,1)}), bf16[32,16,128]{2,1,0:T(8,128)(2,1)S(1)}, u32[]{:S(2)}, u32[]{:S(2)}) async-start(bf16[32,16,128]{2,1,0:T(8,128)(2,1)} %prefix.1), calls=%async_computation.1 | async-start | bytes 262144 | tf_op jit(solution)/shard_map/all_to_all | solution.py:27
  40.1 7.3 %collective-permute-start.1 = (bf16[32,16,128]{2,1,0:T(8,128)(2,1)S(1)}, bf16[32,16,128]{2,1,0:T(8,128)(2,1)S(1)}, u32[]{:S(2)}, u32[]{:S(2)}) collective-permute-start(bf16[32,16,128]{2,1,0:T(8,128)(2,1)S(1)} %all-to-all-done.1), channel_id=1, source_target_pairs={{0,4},{4,0},{1,5},{5,1},{2,6},{6,2},{3,7},{7,3},{8,12},{12,8},{9,1... | collective-permute-start | bytes 393224 | tf_op jit(solution)/shard_map/ppermute | solution.py:23
  44.5 3.7 %copy-start = (f32[768]{0:T(1024)S(1)}, f32[768]{0:T(1024)}, u32[]{:S(2)}) copy-start(f32[768]{0:T(1024)} %gain.3) | copy-start | bytes 9220
  47.4 0.8 copy-start.2
